TPU v7x, 256 devices: a whole 4x4x8 slice. The times are simulated.
256 devices in a mesh: pipe: 16 (over z_lo, x, core), ctx: 16 (over y, z_hi).
Axes of the slice: x: 4, y: 4, z: 8 (z_hi: 4, z_lo: 2; z = z_hi * 2 + z_lo), core: 2. Of those that a mesh axis runs over, the one named last changes fastest.
Arguments:
- queries: bfloat16 [2, 16, 2048, 2560], P(None, 'pipe', 'ctx'), may hold values from -80 to 80
- keys: bfloat16 [2, 16, 2048, 512], P(None, 'pipe', 'ctx'), may hold values from -25 to 25
- values: bfloat16 [2, 16, 2048, 512], P(None, 'pipe', 'ctx'), may hold values from -6 to 6
- grad_a: bfloat16 [16, 2048, 2560], P('pipe', 'ctx'), may hold values from -96 to 96
- grad_b: bfloat16 [16, 2048, 2560], P('pipe', 'ctx'), may hold values from -48 to 48
- imports: int32 [2, 16, 16, 16], P(None, 'pipe'), may hold values from 0 to 1, as said below
- block_ids: int32 [2, 16, 16], P(None, 'pipe'), may hold values from 0 to 15, each once within a row
Outputs:
- dq_a: bfloat16 [16, 2048, 2560], P('pipe', 'ctx')
- dq_b: bfloat16 [16, 2048, 2560], P('pipe', 'ctx')
- kv_grads: bfloat16 [2, 16, 2048, 1024], P(None, 'pipe', 'ctx')
Inputs may be any that keep to these rules, and one draw needn't show every extreme that they name: Every file block sees itself and imports at most 7 other blocks; in each micro-batch and section some block imports exactly 7.
All inputs are finite; a program needn't handle non-finite values.
Results may differ from a plain program's by a relative error of at most 0.015.
Values may be sent and summed in bfloat16 or wider, within the bound.
A program may use at most 64 MiB of HBM per device.

v0:
```python
import math
import jax
import jax.numpy as jnp
from jax import lax
from jax.sharding import PartitionSpec as P

QUERY_HEADS = 20
KEY_VALUE_HEADS = 4
HEAD_DIMENSION = 128
FILE_BLOCK_SIZE = 128
MICRO_BATCHES = 2
negative_large = -1e30


def passed_along(block, axis, distance):
    devices = range(lax.axis_size(axis))
    route = [(i - distance, i) for i in devices if i - distance in devices]
    return lax.ppermute(block, axis, route)


def slot_table(import_mask, block_order):
    blocks_all = block_order.shape[0]
    onehot = (block_order[:, None] == jnp.arange(blocks_all, dtype=jnp.int32)[None, :]).astype(
        jnp.float32
    )
    mapped = jnp.dot(onehot, import_mask.astype(jnp.float32), precision=lax.Precision.HIGHEST)
    return jnp.dot(mapped, onehot.T, precision=lax.Precision.HIGHEST)


def frame_setup(slot_mask, query_start, row_total):
    row_index = query_start + jnp.arange(row_total, dtype=jnp.int32)
    query_slots = row_index // FILE_BLOCK_SIZE
    onehot = (
        query_slots[:, None] == jnp.arange(slot_mask.shape[0], dtype=jnp.int32)[None, :]
    ).astype(jnp.float32)
    reachable = jnp.dot(onehot, slot_mask, precision=lax.Precision.HIGHEST)
    return (reachable, query_slots, row_index % FILE_BLOCK_SIZE)


def tile_mask(frame_info, key_start, key_total_count):
    reachable, query_slots, query_place = frame_info
    key_index = key_start + jnp.arange(key_total_count, dtype=jnp.int32)
    key_slots = key_index // FILE_BLOCK_SIZE
    onehot_keys = (
        key_slots[:, None] == jnp.arange(reachable.shape[1], dtype=jnp.int32)[None, :]
    ).astype(jnp.float32)
    allowed_slot = jnp.dot(reachable, onehot_keys.T, precision=lax.Precision.HIGHEST) > 0.5
    same_slot = query_slots[:, None] == key_slots[None, :]
    causal = (key_index % FILE_BLOCK_SIZE)[None, :] <= query_place[:, None]
    return allowed_slot & (jnp.logical_not(same_slot) | causal)


def over_piece(step_fn, carried, pieces):
    key_fragment, value_fragment = pieces
    piece_rows = key_fragment.shape[0]

    def loop_turn(turn_index, carry_state):
        key_block = lax.dynamic_slice_in_dim(
            key_fragment, turn_index * FILE_BLOCK_SIZE, FILE_BLOCK_SIZE, 0
        )
        value_block = lax.dynamic_slice_in_dim(
            value_fragment, turn_index * FILE_BLOCK_SIZE, FILE_BLOCK_SIZE, 0
        )
        return step_fn(carry_state, key_block, value_block, turn_index * FILE_BLOCK_SIZE)

    return lax.fori_loop(0, piece_rows // FILE_BLOCK_SIZE, loop_turn, carried)


def micro_pass(query_row_tensor, key_rows, value_rows, incoming_gradient, slot_mask, query_start):
    row_total = query_row_tensor.shape[0]
    query_group_width = QUERY_HEADS // KEY_VALUE_HEADS
    softmax_scale = 1.0 / math.sqrt(HEAD_DIMENSION)
    query_head_tensor = query_row_tensor.reshape(
        row_total, KEY_VALUE_HEADS, query_group_width, HEAD_DIMENSION
    )
    gradient_heads = incoming_gradient.reshape(
        row_total, KEY_VALUE_HEADS, query_group_width, HEAD_DIMENSION
    )
    frame_info = frame_setup(slot_mask, query_start, row_total)
    overall_rows = slot_mask.shape[0] * FILE_BLOCK_SIZE

    def stat_step(carried, key_fragment, value_fragment, key_start):
        key_total_count = key_fragment.shape[0]
        allowed = tile_mask(frame_info, key_start, key_total_count)

        def stat_compute_tile(carry_state):
            running_max, running_sum, weighted = carry_state
            key_head_tensor = key_fragment.reshape(key_total_count, KEY_VALUE_HEADS, HEAD_DIMENSION)
            value_head_tensor = value_fragment.reshape(
                key_total_count, KEY_VALUE_HEADS, HEAD_DIMENSION
            )
            scores = (
                jnp.einsum(
                    "rhgd,khd->hgrk",
                    query_head_tensor,
                    key_head_tensor,
                    preferred_element_type=jnp.float32,
                )
                * softmax_scale
            )
            masked = jnp.where(allowed, scores, negative_large)
            new_max = jnp.maximum(running_max, jnp.max(masked, axis=-1))
            weights = jnp.where(allowed, jnp.exp(masked - new_max[..., None]), 0.0)
            rescale = jnp.exp(running_max - new_max)
            running_sum = running_sum * rescale + jnp.sum(weights, axis=-1)
            added = jnp.einsum(
                "hgrk,khd->rhgd",
                weights.astype(jnp.bfloat16),
                value_head_tensor,
                preferred_element_type=jnp.float32,
            )
            weighted = weighted * jnp.transpose(rescale, (2, 0, 1))[..., None] + added
            return (new_max, running_sum, weighted)

        return lax.cond(
            jnp.any(allowed), stat_compute_tile, lambda carry_state: carry_state, carried
        )

    stat_start = (
        jnp.full((KEY_VALUE_HEADS, query_group_width, row_total), negative_large, jnp.float32),
        jnp.zeros((KEY_VALUE_HEADS, query_group_width, row_total), jnp.float32),
        jnp.zeros((row_total, KEY_VALUE_HEADS, query_group_width, HEAD_DIMENSION), jnp.float32),
    )
    stats = over_piece(
        stat_step,
        stat_start,
        (
            lax.all_gather(key_rows, "ctx", axis=0, tiled=True),
            lax.all_gather(value_rows, "ctx", axis=0, tiled=True),
        ),
    )
    running_max, running_sum, weighted = stats
    attended = weighted / jnp.transpose(running_sum, (2, 0, 1))[..., None]
    log_total = running_max + jnp.log(running_sum)
    delta = jnp.transpose(
        jnp.sum(gradient_heads.astype(jnp.float32) * attended, axis=-1), (1, 2, 0)
    )

    def grad_step(carried, key_fragment, value_fragment, key_start):
        key_total_count = key_fragment.shape[0]
        allowed = tile_mask(frame_info, key_start, key_total_count)

        def grad_compute_tile(carry_state):
            q_grad, kv_sums = carry_state
            key_head_tensor = key_fragment.reshape(key_total_count, KEY_VALUE_HEADS, HEAD_DIMENSION)
            value_head_tensor = value_fragment.reshape(
                key_total_count, KEY_VALUE_HEADS, HEAD_DIMENSION
            )
            scores = (
                jnp.einsum(
                    "rhgd,khd->hgrk",
                    query_head_tensor,
                    key_head_tensor,
                    preferred_element_type=jnp.float32,
                )
                * softmax_scale
            )
            probs = jnp.where(
                allowed,
                jnp.exp(jnp.where(allowed, scores - log_total[..., None], negative_large)),
                0.0,
            )
            value_gradient = jnp.einsum(
                "hgrk,rhgd->khd",
                probs.astype(jnp.bfloat16),
                gradient_heads,
                preferred_element_type=jnp.float32,
            )
            prob_grad = jnp.einsum(
                "rhgd,khd->hgrk",
                gradient_heads,
                value_head_tensor,
                preferred_element_type=jnp.float32,
            )
            score_grad = (probs * (prob_grad - delta[..., None])).astype(jnp.bfloat16)
            q_grad = q_grad + jnp.einsum(
                "hgrk,khd->rhgd", score_grad, key_head_tensor, preferred_element_type=jnp.float32
            )
            key_gradient = (
                jnp.einsum(
                    "hgrk,rhgd->khd",
                    score_grad,
                    query_head_tensor,
                    preferred_element_type=jnp.float32,
                )
                * softmax_scale
            )
            update_rows = jnp.concatenate(
                [
                    key_gradient.reshape(key_total_count, KEY_VALUE_HEADS * HEAD_DIMENSION),
                    value_gradient.reshape(key_total_count, KEY_VALUE_HEADS * HEAD_DIMENSION),
                ],
                axis=1,
            )
            previous = lax.dynamic_slice_in_dim(kv_sums, key_start, key_total_count, 0)
            kv_sums = lax.dynamic_update_slice_in_dim(kv_sums, previous + update_rows, key_start, 0)
            return (q_grad, kv_sums)

        return lax.cond(
            jnp.any(allowed), grad_compute_tile, lambda carry_state: carry_state, carried
        )

    grad_start = (
        jnp.zeros((row_total, KEY_VALUE_HEADS, query_group_width, HEAD_DIMENSION), jnp.float32),
        jnp.zeros((overall_rows, 2 * KEY_VALUE_HEADS * HEAD_DIMENSION), jnp.float32),
    )
    q_grad, kv_sums = over_piece(
        grad_step,
        grad_start,
        (
            lax.all_gather(key_rows, "ctx", axis=0, tiled=True),
            lax.all_gather(value_rows, "ctx", axis=0, tiled=True),
        ),
    )
    returned = lax.psum_scatter(
        kv_sums.astype(jnp.bfloat16), "ctx", scatter_dimension=0, tiled=True
    )
    q_result = (
        (q_grad * softmax_scale)
        .reshape(row_total, QUERY_HEADS * HEAD_DIMENSION)
        .astype(jnp.bfloat16)
    )
    return (q_result, returned)


def on_device(queries, keys, values, grad_a, grad_b, imports, block_ids):
    row_total = queries.shape[2]
    query_start = lax.axis_index("ctx") * row_total
    outputs = []
    kv_results = []
    incoming_gradient = grad_a[0]
    for micro_index in range(MICRO_BATCHES):
        if micro_index > 0:
            arrived = passed_along(outputs[0], "pipe", -1)
            incoming_gradient = (
                grad_b[0].astype(jnp.float32) + arrived.astype(jnp.float32)
            ).astype(jnp.bfloat16)
        slot_mask = slot_table(imports[micro_index, 0], block_ids[micro_index, 0])
        q_result, kv_result = micro_pass(
            queries[micro_index, 0],
            keys[micro_index, 0],
            values[micro_index, 0],
            incoming_gradient,
            slot_mask,
            query_start,
        )
        outputs.append(q_result)
        kv_results.append(kv_result)
    return (outputs[0][None], outputs[1][None], jnp.stack(kv_results)[:, None])


def solution(mesh):
    return jax.shard_map(
        on_device,
        mesh=mesh,
        in_specs=(
            P(None, "pipe", "ctx", None),
            P(None, "pipe", "ctx", None),
            P(None, "pipe", "ctx", None),
            P("pipe", "ctx", None),
            P("pipe", "ctx", None),
            P(None, "pipe", None, None),
            P(None, "pipe", None),
        ),
        out_specs=(P("pipe", "ctx", None), P("pipe", "ctx", None), P(None, "pipe", "ctx", None)),
        check_vma=False,
    )
```

profile of v0, /device:TPU:4, one launch (start us, length us, event | category | flops | bytes accessed | tf_op | source)
XLA Modules:
  0.0 529.2 jit_solution(5274312944231669213)
XLA Ops:
  19.5 56.7 %all-gather.9.cloned.1.call-done = bf16[1,1,2048,512]{2,3,1,0:T(8,128)(2,1)} async-done(((bf16[1,1,128,512]{2,3,1,0:T(8,128)(2,1)}), bf16[1,1,2048,512]{2,3,1,0:T(8,128)(2,1)}) %all-gather.9.cloned.1.call-update) | async-done | bytes 2097168 | tf_op jit(solution)/shard_map/all_gather | solution.py:211
  76.2 62.1 %all-gather.11.cloned.1.call-done = bf16[1,1,2048,512]{2,3,1,0:T(8,128)(2,1)} async-done(((bf16[1,1,128,512]{2,3,1,0:T(8,128)(2,1)}), bf16[1,1,2048,512]{2,3,1,0:T(8,128)(2,1)}) %all-gather.11.cloned.1.call-update) | async-done | bytes 2097168 | tf_op jit(solution)/shard_map/all_gather | solution.py:212
  138.4 40.5 %while.80 = (s32[]{:T(128)}, f32[4,5,128]{2,1,0:T(8,128)S(1)}, f32[4,5,128]{2,1,0:T(8,128)S(1)}, f32[128,4,5,128]{3,0,2,1:T(8,128)S(1)}, f32[128,16]{0,1:T(8,128...) while((s32[]{:T(128)}, f32[4,5,128]{2,1,0:T(8,128)S(1)}, ...), condition=%wide.region_6.7_spmd.clone.clone, body=%wide.region_0.6_spmd.clone.clone.sunk | while | flops 174651904 | bytes 8237349 | solution.py:66
  140.0 3.7 conditional.16
  151.7 3.7 conditional.16
  166.7 3.7 conditional.16
  175.2 3.7 conditional.16
  182.1 4.3 broadcast.931.clone
  186.5 46.3 %while.81 = (s32[]{:T(128)}, f32[128,4,5,128]{3,0,2,1:T(8,128)S(1)}, f32[2048,1024]{0,1:T(8,128)}, f32[128,16]{0,1:T(8,128)S(1)}, bf16[2048,512]{0,1:T(8,128)(2,...) while((s32[]{:T(128)}, ...), condition=%wide.region_12.13_spmd.clone.clone, body=%wide.region_8.12_spmd.clone.clone.sunk | while | flops 425974784 | bytes 14221625 | solution.py:66
  188.0 5.2 conditional.17
  201.2 5.2 conditional.17
  217.5 5.2 conditional.17
  227.5 5.2 conditional.17
  234.2 2.4 multiply_convert_fusion.1
  238.6 24.7 %all-gather.15.cloned.1.call-done = bf16[1,1,2048,512]{2,3,1,0:T(8,128)(2,1)} async-done(((bf16[1,1,128,512]{2,3,1,0:T(8,128)(2,1)}), bf16[1,1,2048,512]{2,3,1,0:T(8,128)(2,1)}) %all-gather.15.cloned.1.call-update) | async-done | bytes 2097168 | tf_op jit(solution)/shard_map/all_gather | solution.py:212
  263.4 28.2 %while.82 = (s32[]{:T(128)}, f32[4,5,128]{2,1,0:T(8,128)S(1)}, f32[4,5,128]{2,1,0:T(8,128)S(1)}, f32[128,4,5,128]{3,0,2,1:T(8,128)S(1)}, f32[128,16]{0,1:T(8,128...) while((s32[]{:T(128)}, f32[4,5,128]{2,1,0:T(8,128)S(1)}, ...), condition=%wide.region_19.20_spmd.clone.clone, body=%wide.region_13.0_spmd.clone.clone.sunk | while | flops 174651904 | bytes 8237349 | solution.py:66
  265.0 2.6 conditional.18
  292.0 7.3 %copy.70 = bf16[2048,1024]{1,0:T(8,128)(2,1)} copy(f32[2048,1024]{0,1:T(8,128)} %get-tuple-element.1589) | data formatting | bytes 12582912 | tf_op jit(solution)/shard_map/while | solution.py:66
  302.0 4.3 broadcast.931
  306.4 30.7 %while.83 = (s32[]{:T(128)}, f32[128,4,5,128]{3,0,2,1:T(8,128)S(1)}, f32[2048,1024]{0,1:T(8,128)}, f32[128,16]{0,1:T(8,128)S(1)}, bf16[2048,512]{0,1:T(8,128)(2,...) while((s32[]{:T(128)}, ...), condition=%wide.region_25.26_spmd.clone.clone, body=%wide.region_21.25_spmd.clone.clone.sunk | while | flops 425974784 | bytes 14221625 | solution.py:66
  307.9 5.2 conditional.19
  337.1 7.3 %copy.71 = bf16[2048,1024]{1,0:T(8,128)(2,1)} copy(f32[2048,1024]{0,1:T(8,128)} %get-tuple-element.1590) | data formatting | bytes 12582912 | tf_op jit(solution)/shard_map/while | solution.py:66
  348.3 73.8 %reduce-scatter.3.cloned.1.call-done = bf16[128,1024]{1,0:T(8,128)(2,1)} async-done(((bf16[2048,1024]{1,0:T(8,128)(2,1)}), bf16[128,1024]{1,0:T(8,128)(2,1)}) %reduce-scatter.3.cloned.1.call-update) | async-done | bytes 262160 | tf_op jit(solution)/shard_map/reduce_scatter | solution.py:215
  422.0 98.4 %reduce-scatter.5.cloned.1.call-done = bf16[128,1024]{1,0:T(8,128)(2,1)} async-done(((bf16[2048,1024]{1,0:T(8,128)(2,1)}), bf16[128,1024]{1,0:T(8,128)(2,1)}) %reduce-scatter.5.cloned.1.call-update) | async-done | bytes 262160 | tf_op jit(solution)/shard_map/reduce_scatter | solution.py:215
  (385 shorter events, 129.0 us)
Async XLA Ops:
  7.2 5.4 %copy-start.4 = (s32[2,1,16]{2,1,0:T(1,128)S(1)}, s32[2,1,16]{2,1,0:T(1,128)}, u32[]{:S(2)}) copy-start(s32[2,1,16]{2,1,0:T(1,128)} %param.29) | copy-start | bytes 388
  7.2 5.4 %copy-start.5 = (s32[2,1,16,16]{3,2,1,0:T(8,128)S(1)}, s32[2,1,16,16]{3,2,1,0:T(8,128)}, u32[]{:S(2)}) copy-start(s32[2,1,16,16]{3,2,1,0:T(8,128)} %param.28) | copy-start | bytes 6148
  7.2 69.0 %all-gather.9.cloned.1.call-start = ((), (), s32[]{:S(2)}) async-start(), calls=%async_computation.4 | async-start | bytes 2228224 | tf_op jit(solution)/shard_map/all_gather | solution.py:211
  8.2 5.6 %copy-start.2 = (bf16[1,128,2560]{2,1,0:T(8,128)(2,1)S(1)}, bf16[1,128,2560]{2,1,0:T(8,128)(2,1)}, u32[]{:S(2)}) copy-start(bf16[1,128,2560]{2,1,0:T(8,128)(2,1)} %param.26) | copy-start | bytes 1966084
  9.0 129.3 %all-gather.11.cloned.1.call-start = ((), (), s32[]{:S(2)}) async-start(), calls=%async_computation.5 | async-start | bytes 2228224 | tf_op jit(solution)/shard_map/all_gather | solution.py:212
  10.8 3.4 copy-start.3
  10.8 227.7 %all-gather.13.cloned.1.call-start = ((), (), s32[]{:S(2)}) async-start(), calls=%async_computation.6 | async-start | bytes 2228224 | tf_op jit(solution)/shard_map/all_gather | solution.py:211
  11.7 251.6 %all-gather.15.cloned.1.call-start = ((), (), s32[]{:S(2)}) async-start(), calls=%async_computation.7 | async-start | bytes 2228224 | tf_op jit(solution)/shard_map/all_gather | solution.py:212
  12.5 409.6 %reduce-scatter.3.cloned.1.call-start = ((), (), s32[]{:S(2)}) async-start(), calls=%async_computation.2 | async-start | bytes 4456448 | tf_op jit(solution)/shard_map/reduce_scatter | solution.py:215
  234.2 29.2 %copy-start = (bf16[128,4,5,128]{3,0,2,1:T(8,128)(2,1)S(1)}, bf16[128,4,5,128]{3,0,2,1:T(8,128)(2,1)}, u32[]{:S(2)}) copy-start(bf16[128,4,5,128]{3,0,2,1:T(8,128)(2,1)} %copy.66) | copy-start | bytes 1966084
  236.6 63.0 %collective-permute-start = (bf16[128,2560]{0,1:T(8,128)(2,1)}, bf16[128,2560]{0,1:T(8,128)(2,1)}, u32[]{:S(2)}, u32[]{:S(2)}) collective-permute-start(bf16[128,2560]{0,1:T(8,128)(2,1)} %bitcast.61), channel_id=1, source_target_pairs={{16,0},{32,16},{48,32},{64,48},{80,64},{96,80},{112,96},{128,112},... | collective-permute-start | bytes 1966088 | tf_op jit(solution)/shard_map/ppermute | solution.py:18
  299.3 1.1 copy-start.1
  299.3 221.1 %reduce-scatter.5.cloned.1.call-start = ((), (), s32[]{:S(2)}) async-start(), calls=%async_computation.3 | async-start | bytes 4456448 | tf_op jit(solution)/shard_map/reduce_scatter | solution.py:215
Sparse Core Ops, SparseCore 0:
  11.0 65.1 all-gather.8
  78.6 59.6 all-gather.10
  140.7 59.8 all-gather.12
  202.8 60.3 all-gather.14
  299.5 122.5 reduce-scatter.2
  425.5 94.8 reduce-scatter.4
where the time goes:
time: 532 us; the launch traced here: 529 us
  waiting for transfers between devices  316 us (59%)
  matrix products  79 us (15%)
  local copies, waits for them, and re-layouts  52.4 us (10%)
  loops' own time  45.2 us (8%)
  other arithmetic  20.2 us (4%)
  between operations  14.4 us (3%)
    reduce_scatter x2, waiting for transfers between devices, micro_pass(): lax.psum_scatter(kv_sums.astype(jnp.bfloat16), 'ctx', scatter_dimension=0...  172 us
    all_gather x2, waiting for transfers between devices, micro_pass(): lax.all_gather(value_rows, 'ctx', axis=0, tiled=True)  86.8 us
    all_gather x2, waiting for transfers between devices, micro_pass(): lax.all_gather(key_rows, 'ctx', axis=0, tiled=True)  56.7 us
    dot_general x64, matrix products, tile_mask(): jnp.dot(reachable, onehot_keys.T, precision=lax.Precision.HIGHEST) > 0.5  55.8 us
    another operation x4, loops' own time, over_piece(): return lax.fori_loop(0, piece_rows // FILE_BLOCK_SIZE, loop_turn, carried)  43.8 us
    while x6, local copies, waits for them, and re-layouts, over_piece(): return lax.fori_loop(0, piece_rows // FILE_BLOCK_SIZE, loop_turn, carried)  18.5 us
    unnamed x22, local copies, waits for them, and re-layouts  10.7 us
  transfers between devices with their start and end apart: 7, of which 5 were waited for; matrix products, arithmetic and copies ran while one was open for 28% of the time, Pallas kernels for 0%

commit v1 on v0

--- a/solution.py
+++ b/solution.py
@@ -3,6 +3,7 @@
 import jax.numpy as jnp
 from jax import lax
 from jax.sharding import PartitionSpec as P
+from jax.lax import all_to_all, axis_size
 
 QUERY_HEADS = 20
 KEY_VALUE_HEADS = 4
@@ -10,6 +11,14 @@
 FILE_BLOCK_SIZE = 128
 MICRO_BATCHES = 2
 negative_large = -1e30
+
+
+def check_pages(row_data, mesh_name, array_axis):
+    val2 = axis_size(mesh_name)
+    x_next = jnp.stack([row_data] * val2)
+    known = all_to_all(x_next, axis_name=mesh_name, split_axis=0, concat_axis=0)
+    val = jnp.concatenate(known, axis=array_axis)
+    return val
 
 
 def passed_along(block, axis, distance):
@@ -207,10 +216,7 @@
     q_grad, kv_sums = over_piece(
         grad_step,
         grad_start,
-        (
-            lax.all_gather(key_rows, "ctx", axis=0, tiled=True),
-            lax.all_gather(value_rows, "ctx", axis=0, tiled=True),
-        ),
+        (check_pages(key_rows, "ctx", 0), lax.all_gather(value_rows, "ctx", axis=0, tiled=True)),
     )
     returned = lax.psum_scatter(
         kv_sums.astype(jnp.bfloat16), "ctx", scatter_dimension=0, tiled=True

time: 532 us -> 578 us (1.086)
  starting transfers between devices: 2.34 us -> 32.5 us
  local copies, waits for them, and re-layouts: 52.4 us -> 70.5 us
    all_to_all x0 -> x2, starting transfers between devices: none -> 30.2 us  [check_pages(): known = all_to_all(x_next, axis_name=mesh_name, split_axis=0, concat_axis=0)]
    reduce_scatter x2, waiting for transfers between devices: 172 us -> 161 us  [micro_pass(): lax.psum_scatter(kv_sums.astype(jnp.bfloat16), 'ctx', scatter_dimension=0...]
    all_gather x2, waiting for transfers between devices: 56.7 us -> 67.1 us  [micro_pass(): lax.all_gather(key_rows, 'ctx', axis=0, tiled=True)]
    unnamed x22 -> x32, local copies, waits for them, and re-layouts: 10.7 us -> 17.6 us
    all_to_all x0 -> x2, local copies, waits for them, and re-layouts: none -> 6.79 us  [check_pages(): known = all_to_all(x_next, axis_name=mesh_name, split_axis=0, concat_axis=0)]
    another operation x10 -> x12, local copies, waits for them, and re-layouts: 9.18 us -> 12.7 us
  transfers between devices with their start and end apart: 7 -> 9, of which waited for: 5 -> 5; matrix products, arithmetic and copies ran while one was open for 28% -> 29% of each run, Pallas kernels for 0% -> 0%
where the time goes in v1:
time: 578 us; the launch traced here: 575 us
  waiting for transfers between devices  313 us (54%)
  matrix products  79.6 us (14%)
  local copies, waits for them, and re-layouts  70.5 us (12%)
  loops' own time  45.9 us (8%)
  starting transfers between devices  32.5 us (6%)
  other arithmetic  18.8 us (3%)
  between operations  14.4 us (2%)
    reduce_scatter x2, waiting for transfers between devices, micro_pass(): lax.psum_scatter(kv_sums.astype(jnp.bfloat16), 'ctx', scatter_dimension=0...  161 us
    all_gather x2, waiting for transfers between devices, micro_pass(): lax.all_gather(value_rows, 'ctx', axis=0, tiled=True)  84.7 us
    all_gather x2, waiting for transfers between devices, micro_pass(): lax.all_gather(key_rows, 'ctx', axis=0, tiled=True)  67.1 us
    dot_general x64, matrix products, tile_mask(): jnp.dot(reachable, onehot_keys.T, precision=lax.Precision.HIGHEST) > 0.5  56.5 us
    another operation x4, loops' own time, over_piece(): return lax.fori_loop(0, piece_rows // FILE_BLOCK_SIZE, loop_turn, carried)  44.4 us
    all_to_all x2, starting transfers between devices, check_pages(): known = all_to_all(x_next, axis_name=mesh_name, split_axis=0, concat_axis=0)  30.2 us
    while x6, local copies, waits for them, and re-layouts, over_piece(): return lax.fori_loop(0, piece_rows // FILE_BLOCK_SIZE, loop_turn, carried)  19.4 us
    unnamed x32, local copies, waits for them, and re-layouts  17.6 us
  transfers between devices with their start and end apart: 9, of which 5 were waited for; matrix products, arithmetic and copies ran while one was open for 29% of the time, Pallas kernels for 0%

profile of v1, /device:TPU:4, one launch (start us, length us, event | category | flops | bytes accessed | tf_op | source)
XLA Modules:
  0.0 575.2 jit_solution(6376369731054151769)
XLA Ops:
  13.5 11.4 %all-to-all-start = ((bf16[16,128,512]{1,2,0:T(8,128)(2,1)}), bf16[16,128,512]{1,2,0:T(8,128)(2,1)}, u32[]{:S(2)}, u32[]{:S(2)}) async-start(bf16[16,128,512]{1,2,0:T(8,128)(2,1)} %stack.15), calls=%async_computation | async-start | bytes 4194304 | tf_op jit(solution)/shard_map/all_to_all | solution.py:19
  32.7 67.1 %all-gather.9.cloned.1.call-done = bf16[1,1,2048,512]{2,3,1,0:T(8,128)(2,1)} async-done(((bf16[1,1,128,512]{2,3,1,0:T(8,128)(2,1)}), bf16[1,1,2048,512]{2,3,1,0:T(8,128)(2,1)}) %all-gather.9.cloned.1.call-update) | async-done | bytes 2097168 | tf_op jit(solution)/shard_map/all_gather | solution.py:137
  99.8 62.2 %all-gather.11.cloned.1.call-done = bf16[1,1,2048,512]{2,3,1,0:T(8,128)(2,1)} async-done(((bf16[1,1,128,512]{2,3,1,0:T(8,128)(2,1)}), bf16[1,1,2048,512]{2,3,1,0:T(8,128)(2,1)}) %all-gather.11.cloned.1.call-update) | async-done | bytes 2097168 | tf_op jit(solution)/shard_map/all_gather | solution.py:219
  162.1 41.8 %while.80 = (s32[]{:T(128)}, f32[4,5,128]{2,1,0:T(8,128)S(1)}, f32[4,5,128]{2,1,0:T(8,128)S(1)}, f32[128,4,5,128]{3,0,2,1:T(8,128)S(1)}, f32[128,16]{0,1:T(8,128...) while((s32[]{:T(128)}, f32[4,5,128]{2,1,0:T(8,128)S(1)}, ...), condition=%wide.region_6.7_spmd.clone.clone, body=%wide.region_0.6_spmd.clone.clone.sunk | while | flops 174651904 | bytes 8237349 | solution.py:75
  163.8 3.7 conditional.16
  200.2 3.7 conditional.16
  207.2 18.8 %all-to-all-start.1 = ((bf16[16,128,512]{1,2,0:T(8,128)(2,1)}), bf16[16,128,512]{1,2,0:T(8,128)(2,1)}, u32[]{:S(2)}, u32[]{:S(2)}) async-start(bf16[16,128,512]{1,2,0:T(8,128)(2,1)} %stack.16), calls=%async_computation.1 | async-start | bytes 4194304 | tf_op jit(solution)/shard_map/all_to_all | solution.py:19
  226.1 3.9 copy.137
  230.0 4.1 copy.143
  234.5 4.3 broadcast.933.clone
  238.8 46.2 %while.81 = (s32[]{:T(128)}, f32[128,4,5,128]{3,0,2,1:T(8,128)S(1)}, f32[2048,1024]{0,1:T(8,128)}, f32[128,16]{0,1:T(8,128)S(1)}, bf16[2048,512]{0,1:T(8,128)(2,...) while((s32[]{:T(128)}, ...), condition=%wide.region_12.13_spmd.clone.clone, body=%wide.region_8.12_spmd.clone.clone.sunk | while | flops 425974784 | bytes 14221625 | solution.py:75
  240.3 5.2 conditional.17
  253.5 5.2 conditional.17
  269.8 5.2 conditional.17
  279.8 5.2 conditional.17
  291.0 22.5 %all-gather.15.cloned.1.call-done = bf16[1,1,2048,512]{2,3,1,0:T(8,128)(2,1)} async-done(((bf16[1,1,128,512]{2,3,1,0:T(8,128)(2,1)}), bf16[1,1,2048,512]{2,3,1,0:T(8,128)(2,1)}) %all-gather.15.cloned.1.call-update) | async-done | bytes 2097168 | tf_op jit(solution)/shard_map/all_gather | solution.py:219
  313.6 28.2 %while.82 = (s32[]{:T(128)}, f32[4,5,128]{2,1,0:T(8,128)S(1)}, f32[4,5,128]{2,1,0:T(8,128)S(1)}, f32[128,4,5,128]{3,0,2,1:T(8,128)S(1)}, f32[128,16]{0,1:T(8,128...) while((s32[]{:T(128)}, f32[4,5,128]{2,1,0:T(8,128)S(1)}, ...), condition=%wide.region_19.20_spmd.clone.clone, body=%wide.region_13.0_spmd.clone.clone.sunk | while | flops 174651904 | bytes 8237349 | solution.py:75
  348.7 7.3 %copy.154 = bf16[2048,1024]{1,0:T(8,128)(2,1)} copy(f32[2048,1024]{0,1:T(8,128)} %get-tuple-element.1589) | data formatting | bytes 12582912 | tf_op jit(solution)/shard_map/while | solution.py:75
  358.7 4.3 broadcast.933
  363.1 30.7 %while.83 = (s32[]{:T(128)}, f32[128,4,5,128]{3,0,2,1:T(8,128)S(1)}, f32[2048,1024]{0,1:T(8,128)}, f32[128,16]{0,1:T(8,128)S(1)}, bf16[2048,512]{0,1:T(8,128)(2,...) while((s32[]{:T(128)}, ...), condition=%wide.region_25.26_spmd.clone.clone, body=%wide.region_21.25_spmd.clone.clone.sunk | while | flops 425974784 | bytes 14221625 | solution.py:75
  364.6 5.2 conditional.19
  393.7 7.3 %copy.155 = bf16[2048,1024]{1,0:T(8,128)(2,1)} copy(f32[2048,1024]{0,1:T(8,128)} %get-tuple-element.1590) | data formatting | bytes 12582912 | tf_op jit(solution)/shard_map/while | solution.py:75
  405.0 63.6 %reduce-scatter.3.cloned.1.call-done = bf16[128,1024]{1,0:T(8,128)(2,1)} async-done(((bf16[2048,1024]{1,0:T(8,128)(2,1)}), bf16[128,1024]{1,0:T(8,128)(2,1)}) %reduce-scatter.3.cloned.1.call-update) | async-done | bytes 262160 | tf_op jit(solution)/shard_map/reduce_scatter | solution.py:221
  468.6 97.9 %reduce-scatter.5.cloned.1.call-done = bf16[128,1024]{1,0:T(8,128)(2,1)} async-done(((bf16[2048,1024]{1,0:T(8,128)(2,1)}), bf16[128,1024]{1,0:T(8,128)(2,1)}) %reduce-scatter.5.cloned.1.call-update) | async-done | bytes 262160 | tf_op jit(solution)/shard_map/reduce_scatter | solution.py:221
  (403 shorter events, 151.0 us)
Async XLA Ops:
  7.2 92.6 %all-gather.9.cloned.1.call-start = ((), (), s32[]{:S(2)}) async-start(), calls=%async_computation.6 | async-start | bytes 2228224 | tf_op jit(solution)/shard_map/all_gather | solution.py:137
  9.0 2.7 copy-start.5
  9.0 153.0 %all-gather.11.cloned.1.call-start = ((), (), s32[]{:S(2)}) async-start(), calls=%async_computation.7 | async-start | bytes 2228224 | tf_op jit(solution)/shard_map/all_gather | solution.py:219
  10.8 280.2 %all-gather.13.cloned.1.call-start = ((), (), s32[]{:S(2)}) async-start(), calls=%async_computation.8 | async-start | bytes 2228224 | tf_op jit(solution)/shard_map/all_gather | solution.py:137
  13.5 12.3 %copy-start.8 = (s32[2,1,16]{2,1,0:T(1,128)S(1)}, s32[2,1,16]{2,1,0:T(1,128)}, u32[]{:S(2)}) copy-start(s32[2,1,16]{2,1,0:T(1,128)} %param.29) | copy-start | bytes 388
  13.5 12.3 %copy-start.9 = (s32[2,1,16,16]{3,2,1,0:T(8,128)S(1)}, s32[2,1,16,16]{3,2,1,0:T(8,128)}, u32[]{:S(2)}) copy-start(s32[2,1,16,16]{3,2,1,0:T(8,128)} %param.28) | copy-start | bytes 6148
  13.5 13.5 %copy-start.6 = (bf16[1,128,2560]{2,1,0:T(8,128)(2,1)S(1)}, bf16[1,128,2560]{2,1,0:T(8,128)(2,1)}, u32[]{:S(2)}) copy-start(bf16[1,128,2560]{2,1,0:T(8,128)(2,1)} %param.26) | copy-start | bytes 1966084
  13.5 192.0 %all-to-all-start = ((bf16[16,128,512]{1,2,0:T(8,128)(2,1)}), bf16[16,128,512]{1,2,0:T(8,128)(2,1)}, u32[]{:S(2)}, u32[]{:S(2)}) async-start(bf16[16,128,512]{1,2,0:T(8,128)(2,1)} %stack.15), calls=%async_computation | async-start | bytes 4194304 | tf_op jit(solution)/shard_map/all_to_all | solution.py:19
  24.9 2.5 copy-start.7
  24.9 288.6 %all-gather.15.cloned.1.call-start = ((), (), s32[]{:S(2)}) async-start(), calls=%async_computation.9 | async-start | bytes 2228224 | tf_op jit(solution)/shard_map/all_gather | solution.py:219
  204.0 1.5 copy-start.4
  207.2 136.1 %all-to-all-start.1 = ((bf16[16,128,512]{1,2,0:T(8,128)(2,1)}), bf16[16,128,512]{1,2,0:T(8,128)(2,1)}, u32[]{:S(2)}, u32[]{:S(2)}) async-start(bf16[16,128,512]{1,2,0:T(8,128)(2,1)} %stack.16), calls=%async_computation.1 | async-start | bytes 4194304 | tf_op jit(solution)/shard_map/all_to_all | solution.py:19
  226.0 242.5 %reduce-scatter.3.cloned.1.call-start = ((), (), s32[]{:S(2)}) async-start(), calls=%async_computation.4 | async-start | bytes 4456448 | tf_op jit(solution)/shard_map/reduce_scatter | solution.py:221
  230.0 4.1 copy-start.2
  286.5 27.1 %copy-start = (bf16[128,4,5,128]{3,0,2,1:T(8,128)(2,1)S(1)}, bf16[128,4,5,128]{3,0,2,1:T(8,128)(2,1)}, u32[]{:S(2)}) copy-start(bf16[128,4,5,128]{3,0,2,1:T(8,128)(2,1)} %copy.149) | copy-start | bytes 1966084
  288.9 67.2 %collective-permute-start = (bf16[128,2560]{0,1:T(8,128)(2,1)}, bf16[128,2560]{0,1:T(8,128)(2,1)}, u32[]{:S(2)}, u32[]{:S(2)}) collective-permute-start(bf16[128,2560]{0,1:T(8,128)(2,1)} %bitcast.65), channel_id=1, source_target_pairs={{16,0},{32,16},{48,32},{64,48},{80,64},{96,80},{112,96},{128,112},... | collective-permute-start | bytes 1966088 | tf_op jit(solution)/shard_map/ppermute | solution.py:27
  356.0 1.1 copy-start.3
  356.0 2.3 copy-start.1
  356.0 210.4 %reduce-scatter.5.cloned.1.call-start = ((), (), s32[]{:S(2)}) async-start(), calls=%async_computation.5 | async-start | bytes 4456448 | tf_op jit(solution)/shard_map/reduce_scatter | solution.py:221
Sparse Core Ops, SparseCore 0:
  11.0 88.7 all-gather.8
  102.2 59.7 all-gather.10
  164.4 59.7 all-gather.12
  226.5 86.9 all-gather.14
  356.2 112.3 reduce-scatter.2
  472.0 94.3 reduce-scatter.4
